TPU v7x, 256 devices: a whole 4x4x8 slice. The times are simulated.
256 devices in a mesh: section: 8 (over z_hi, x), rep: 32 (over z_lo, y, core).
Axes of the slice: x: 4, y: 4, z: 8 (z_hi: 2, z_lo: 4; z = z_hi * 4 + z_lo), core: 2. Of those that a mesh axis runs over, the one named last changes fastest.
Arguments:
- layer_in: bfloat16 [8, 128, 4096], P('section', 'rep'), may hold values from -6 to 6
- next_in: bfloat16 [8, 128, 4096], P('section', 'rep'), may hold values from -6 to 6
- returned: bfloat16 [8, 256, 4096], P('section', 'rep'), may hold values from -6 to 6
- norm_gain: float32 [8, 4096], P('section'), may hold values from 0.25 to 1.75
- gate_weight: bfloat16 [8, 4096, 14336], P('section', None, 'rep'), may hold values from -0.09375 to 0.09375
- up_weight: bfloat16 [8, 4096, 14336], P('section', None, 'rep'), may hold values from -0.09375 to 0.09375
- down_weight: bfloat16 [8, 14336, 4096], P('section', 'rep'), may hold values from -0.046875 to 0.046875
- wiring: int32 [8, 32, 32], P('section'), may hold values from 0 to 2, as said below
Outputs:
- forwarded: bfloat16 [8, 256, 4096], P('section', 'rep')
- input_grad: bfloat16 [8, 128, 4096], P('section', 'rep')
- next_out: bfloat16 [8, 128, 4096], P('section', 'rep')
Inputs may be any that keep to these rules, and one draw needn't show every extreme that they name: For every position p and row group r the entries wiring[p, r, :] sum to 2. For every position p and receiver j the column wiring[p, :, j] sums to at most 4, and in every position some column sums to exactly 4. In every position some row group sends all its 2 blocks to one receiver, and some receiver gets none.
All inputs are finite; a program needn't handle non-finite values.
Results may differ from a plain program's by a relative error of at most 0.035.
Values may be sent and summed in bfloat16 or wider, within the bound.
No kernel may reach another device: no remote copies, remote signals or barrier semaphores. Data moves between devices by JAX's collectives and lax.ppermute only.
A program may use at most 128 MiB of HBM per device.

v0:
```python
import jax
import jax.numpy as jnp
from jax import lax
from jax.sharding import PartitionSpec as P

BLK = 2
epsilon = 1e-05
step_rate = 0.5


def passed_along(value, axis, by):
    peers = lax.axis_size(axis)
    return lax.ppermute(value, axis, [(i, (i + by) % peers) for i in range(peers)])


def route_tables(wiring_section, replicas, blocks_dev, capacity):
    row_total = jnp.cumsum(wiring_section, axis=1)
    column_total = jnp.cumsum(wiring_section, axis=0)
    row_start = row_total - wiring_section
    column_start = column_total - wiring_section
    slot_ids = jnp.arange(capacity, dtype=jnp.int32)
    block_ids = jnp.arange(blocks_dev, dtype=jnp.int32)
    member_ids = jnp.arange(replicas, dtype=jnp.int32)
    sender = jnp.sum(
        (column_total.T[:, :, None] <= slot_ids[None, None, :]).astype(jnp.int32), axis=1
    )
    slot_live = slot_ids[None, :] < column_total[replicas - 1][:, None]
    sender = jnp.minimum(sender, replicas - 1)
    within = slot_ids[None, :] - column_start[sender, member_ids[:, None]]
    within = jnp.where(slot_live, within, 0)
    local_source = sender * blocks_dev + within
    global_source = sender * blocks_dev + row_start[sender, member_ids[:, None]] + within
    target_member = jnp.sum(
        (row_total[:, None, :] <= block_ids[None, :, None]).astype(jnp.int32), axis=2
    )
    target_member = jnp.minimum(target_member, replicas - 1)
    block_offset = block_ids[None, :] - row_start[member_ids[:, None], target_member]
    global_target = (
        target_member * capacity + column_start[member_ids[:, None], target_member] + block_offset
    )
    local_target = target_member * blocks_dev + block_offset
    return (
        wiring_section,
        row_start,
        column_start,
        slot_live,
        local_source,
        global_source,
        global_target,
        local_target,
    )


def gather_rows(local_rows):
    return lax.all_gather(local_rows, "rep", axis=0, tiled=True)


def reduce_rows(term_rows):
    return lax.psum_scatter(
        term_rows.astype(jnp.bfloat16), "rep", scatter_dimension=0, tiled=True
    ).astype(jnp.float32)


def route_blocks(buffer_rows):
    return lax.all_to_all(buffer_rows, "rep", split_axis=0, concat_axis=0, tiled=True)


def pass_section(slot_rows, offset_by):
    return passed_along(slot_rows, "section", offset_by)


def normalize(layer_rows, gain_row):
    values = layer_rows.astype(jnp.float32)
    row_scale = lax.rsqrt(jnp.mean(values * values, axis=1, keepdims=True) + epsilon)
    normed_local = (values * row_scale * gain_row[None, :]).astype(jnp.bfloat16)
    return (values, row_scale, gather_rows(normed_local))


def down_terms(hidden, down_local, values, position):
    term_rows = jnp.dot(hidden, down_local, preferred_element_type=jnp.float32)
    row_count = values.shape[0]
    own_part = lax.dynamic_slice_in_dim(term_rows, position * row_count, row_count, 0) + values
    return lax.dynamic_update_slice_in_dim(term_rows, own_part, position * row_count, 0)


def local_forward(layer_rows, gain_row, gate_local, up_local, down_local, position):
    values, row_scale, normed = normalize(layer_rows, gain_row)
    gate_act = jnp.dot(normed, gate_local, preferred_element_type=jnp.float32)
    up_act = jnp.dot(normed, up_local, preferred_element_type=jnp.float32)
    hidden = (jax.nn.silu(gate_act) * up_act).astype(jnp.bfloat16)
    term_rows = down_terms(hidden, down_local, values, position)
    return (term_rows, values, row_scale, normed, gate_act, up_act, hidden)


def values_rows_term(values, row_scale, scaled_grad):
    return values * row_scale**3 * jnp.mean(values * scaled_grad, axis=1, keepdims=True)


def per_device(layer_in, next_in, returned, norm_gain, gate_weight, up_weight, down_weight, wiring):
    replicas = lax.axis_size("rep")
    position = lax.axis_index("rep")
    partner_offset = lax.axis_size("section") // 2
    row_count = layer_in.shape[1]
    feature_count = layer_in.shape[2]
    blocks_dev = row_count // BLK
    capacity = returned.shape[1] // BLK
    token_count = row_count * replicas
    gain_row = norm_gain[0]
    gate_local = gate_weight[0]
    up_local = up_weight[0]
    down_local = down_weight[0]
    zero_value = jnp.zeros((), jnp.bfloat16)
    block_ids = jnp.arange(blocks_dev, dtype=jnp.int32)
    (
        counts,
        row_start,
        column_start,
        slot_live,
        local_source,
        global_source,
        global_target,
        local_target,
    ) = route_tables(wiring[0], replicas, blocks_dev, capacity)
    term_rows, values, row_scale, normed, gate_act, up_act, hidden = local_forward(
        layer_in[0], gain_row, gate_local, up_local, down_local, position
    )
    out_rows = reduce_rows(term_rows).astype(jnp.bfloat16)
    own_blocks = out_rows.reshape(blocks_dev, BLK, feature_count)
    my_start = lax.dynamic_index_in_dim(row_start, position, 0, keepdims=False)
    my_counts = lax.dynamic_index_in_dim(counts, position, 0, keepdims=False)
    pick_index = jnp.minimum(my_start[:, None] + block_ids[None, :], blocks_dev - 1)
    keep_mask = block_ids[None, :] < my_counts[:, None]
    outgoing = jnp.take(own_blocks, pick_index.reshape(-1), axis=0).reshape(
        replicas, blocks_dev, BLK, feature_count
    )
    outgoing = jnp.where(keep_mask[:, :, None, None], outgoing, zero_value)
    incoming = route_blocks(outgoing.reshape(replicas, row_count, feature_count))
    incoming = incoming.reshape(replicas * blocks_dev, BLK, feature_count)
    my_source = lax.dynamic_index_in_dim(local_source, position, 0, keepdims=False)
    my_live = lax.dynamic_index_in_dim(slot_live, position, 0, keepdims=False)
    slot_blocks = jnp.where(
        my_live[:, None, None], jnp.take(incoming, my_source, axis=0), zero_value
    )
    slot_rows = slot_blocks.reshape(capacity * BLK, feature_count)
    forwarded = pass_section(slot_rows, 1)
    later_slots = pass_section(returned[0], -1)
    back_blocks = later_slots.reshape(capacity, BLK, feature_count)
    column_offsets = lax.dynamic_index_in_dim(column_start, position, 1, keepdims=False)
    column_counts = lax.dynamic_index_in_dim(counts, position, 1, keepdims=False)
    pick_back = jnp.minimum(column_offsets[:, None] + block_ids[None, :], capacity - 1)
    keep_back = block_ids[None, :] < column_counts[:, None]
    returning = jnp.take(back_blocks, pick_back.reshape(-1), axis=0).reshape(
        replicas, blocks_dev, BLK, feature_count
    )
    returning = jnp.where(keep_back[:, :, None, None], returning, zero_value)
    arrived = route_blocks(returning.reshape(replicas, row_count, feature_count))
    arrived = arrived.reshape(replicas * blocks_dev, BLK, feature_count)
    my_target = lax.dynamic_index_in_dim(local_target, position, 0, keepdims=False)
    cotangent_own = jnp.take(arrived, my_target, axis=0).reshape(row_count, feature_count)
    cotangent_all = gather_rows(cotangent_own)
    rows_contract = (((0,), (0,)), ((), ()))
    cols_contract = (((1,), (1,)), ((), ()))
    update_factor = step_rate / token_count
    grad_down = lax.dot_general(
        hidden, cotangent_all, rows_contract, preferred_element_type=jnp.float32
    )
    updated_down = (down_local.astype(jnp.float32) - update_factor * grad_down).astype(jnp.bfloat16)
    mate_down = passed_along(updated_down, "section", partner_offset)
    dhidden = lax.dot_general(
        cotangent_all, down_local, cols_contract, preferred_element_type=jnp.float32
    )
    sigmoid_gate = jax.nn.sigmoid(gate_act)
    silu_gate = gate_act * sigmoid_gate
    grad_gate_act = (
        dhidden * up_act * sigmoid_gate * (1.0 + gate_act * (1.0 - sigmoid_gate))
    ).astype(jnp.bfloat16)
    grad_up_act = (dhidden * silu_gate).astype(jnp.bfloat16)
    dterm_rows = lax.dot_general(
        grad_gate_act, gate_local, cols_contract, preferred_element_type=jnp.float32
    )
    dterm_rows = dterm_rows + lax.dot_general(
        grad_up_act, up_local, cols_contract, preferred_element_type=jnp.float32
    )
    dnormed = reduce_rows(dterm_rows)
    scaled_grad = gain_row[None, :] * dnormed
    input_grad = (
        cotangent_own.astype(jnp.float32)
        + row_scale * scaled_grad
        - values_rows_term(values, row_scale, scaled_grad)
    ).astype(jnp.bfloat16)
    grad_gate = lax.dot_general(
        normed, grad_gate_act, rows_contract, preferred_element_type=jnp.float32
    )
    grad_up = lax.dot_general(
        normed, grad_up_act, rows_contract, preferred_element_type=jnp.float32
    )
    updated_gate = (gate_local.astype(jnp.float32) - update_factor * grad_gate).astype(jnp.bfloat16)
    updated_up = (up_local.astype(jnp.float32) - update_factor * grad_up).astype(jnp.bfloat16)
    next_values, next_scale, next_normed = normalize(next_in[0], gain_row)
    own_gate_next = jnp.dot(next_normed, updated_gate, preferred_element_type=jnp.float32)
    own_up_next = jnp.dot(next_normed, updated_up, preferred_element_type=jnp.float32)
    mate_pair = passed_along(jnp.stack((updated_gate, updated_up)), "section", partner_offset)
    mate_gate_next = jnp.dot(next_normed, mate_pair[0], preferred_element_type=jnp.float32)
    mate_up_next = jnp.dot(next_normed, mate_pair[1], preferred_element_type=jnp.float32)
    gate_next = 0.5 * (own_gate_next + mate_gate_next)
    up_next = 0.5 * (own_up_next + mate_up_next)
    hidden_next = (jax.nn.silu(gate_next) * up_next).astype(jnp.bfloat16)
    averaged_down = (
        (updated_down.astype(jnp.float32) + mate_down.astype(jnp.float32)) * 0.5
    ).astype(jnp.bfloat16)
    term_next = down_terms(hidden_next, averaged_down, next_values, position)
    next_rows = reduce_rows(term_next).astype(jnp.bfloat16)
    return (forwarded[None], input_grad[None], next_rows[None])


def solution(mesh):
    in_specs = (
        P("section", "rep", None),
        P("section", "rep", None),
        P("section", "rep", None),
        P("section", None),
        P("section", None, "rep"),
        P("section", None, "rep"),
        P("section", "rep", None),
        P("section", None, None),
    )
    out_specs = (P("section", "rep", None), P("section", "rep", None), P("section", "rep", None))
    return jax.shard_map(
        per_device, mesh=mesh, in_specs=in_specs, out_specs=out_specs, check_vma=False
    )
```

profile of v0, /device:TPU:33, one launch (start us, length us, event | category | flops | bytes accessed | tf_op | source)
XLA Modules:
  0.0 1053.8 jit_solution(2265218487439478688)
XLA Ops:
  7.2 8.3 collective-permute-start.1
  15.4 0.8 reduce_window_sum.22
  16.2 0.9 reduce_window_sum.23
  17.1 0.9 dynamic-slice_reduce_fusion.1
  18.0 0.7 bitcast_subtract_fusion
  19.5 0.9 fusion.27
  20.4 0.9 fusion.23
  21.4 2.7 gather_fusion.4
  24.1 0.4 gather.37
  24.5 1.8 select_select_fusion
  26.3 7.6 all-to-all-start.1
  34.0 0.7 fusion.36
  35.1 0.8 gather_fusion.3
  36.5 24.2 %all-to-all-done.1 = bf16[32,4,4096]{2,1,0:T(4,128)(2,1)S(1)} async-done(((bf16[32,4,4096]{2,1,0:T(4,128)(2,1)}), bf16[32,4,4096]{2,1,0:T(4,128)(2,1)S(1)}, u32[]{:S(2)}, u32[]{:S(2)}) %all-to-all-start.1) | async-done | bytes 1048608 | tf_op jit(solution)/shard_map/all_to_all | solution.py:65
  60.7 0.5 reshape.323
  61.2 0.6 gather_fusion.5
  61.9 0.7 fusion.55
  62.6 0.2 all-gather.11.cloned.1.call-start
  62.8 32.1 %all-gather.7.cloned.1.call-done = bf16[32,4,4096]{2,1,0:T(4,128)(2,1)} async-done(((bf16[1,4,4096]{2,1,0:T(4,128)(2,1)}), bf16[32,4,4096]{2,1,0:T(4,128)(2,1)}) %all-gather.7.cloned.1.call-update) | async-done | bytes 1048592 | tf_op jit(solution)/shard_map/all_gather | solution.py:55
  95.0 1.3 reshape.371
  96.3 3.3 fusion.13
  99.6 1.1 fusion.9
  100.8 53.6 %all-gather.9.cloned.1.call-done = bf16[32,4,4096]{2,1,0:T(4,128)(2,1)} async-done(((bf16[1,4,4096]{2,1,0:T(4,128)(2,1)}), bf16[32,4,4096]{2,1,0:T(4,128)(2,1)}) %all-gather.9.cloned.1.call-update) | async-done | bytes 1048592 | tf_op jit(solution)/shard_map/all_gather | solution.py:55
  154.4 1.3 reshape.373
  155.7 3.3 multiply_convert_fusion.3
  159.1 1.1 subtract_convert_fusion.2
  160.2 0.9 copy-done.7
  161.1 1.1 subtract_convert_fusion.1
  162.2 4.0 pad_maximum_fusion
  166.4 3.7 collective-permute-start.2
  170.1 4.9 subtract_convert_fusion
  175.0 1.7 collective-permute-start.3
  176.7 508.5 %all-gather.11.cloned.1.call-done = bf16[32,4,4096]{2,1,0:T(4,128)(2,1)} async-done(((bf16[1,4,4096]{2,1,0:T(4,128)(2,1)}), bf16[32,4,4096]{2,1,0:T(4,128)(2,1)}) %all-gather.11.cloned.1.call-update) | async-done | bytes 1048592 | tf_op jit(solution)/shard_map/all_gather | solution.py:55
  685.2 1.3 reshape.375
  686.6 2.9 fusion.6
  689.6 1.2 convert_element_type.90
  690.7 1.1 fusion.56
  692.0 1.1 fusion.57
  693.1 0.9 copy-done.5
  694.1 0.8 fusion.11
  694.8 1.3 copy-done.8
  696.1 1.8 fusion
  697.9 3.9 fusion.17
  701.7 6.9 fusion.1
  708.7 1.1 convert_element_type.111
  710.1 0.7 fusion.47
  711.4 1.3 gather_fusion
  712.9 0.6 dynamic-slice.2
  714.2 260.7 %all-reduce.6.cloned.1.call-done = (bf16[128,4096]{1,0:T(8,128)(2,1)}, bf16[128,4096]{1,0:T(8,128)(2,1)}, bf16[128,4096]{1,0:T(8,128)(2,1)}) async-done(((bf16[128,4096]{1,0:T(8,128)(2,1)}, bf16[128,4096]{1,0:T(8,128)(2,1)}, bf16[128,4096]{1,0:T(8,128)(2,1)}), (bf16[128,4096]{1,0:T(8,128)(2,1)}, bf16[128,4096]{1,0:T(8,128)(2,1)}, bf16[128,4096]{1,0:T(8,128)(2,1)})) %all-reduce.6.cloned.1.call-update) | async-done | bytes 3145744
  974.9 0.9 constant_dynamic-slice_fusion.5
  975.8 2.7 gather_fusion.1
  978.4 0.4 gather.32
  978.9 1.7 select_select_fusion.1
  980.6 27.0 %all-to-all-start = ((bf16[32,4,4096]{2,1,0:T(4,128)(2,1)}), bf16[32,4,4096]{2,1,0:T(4,128)(2,1)S(1)}, u32[]{:S(2)}, u32[]{:S(2)}) async-start(bf16[32,4,4096]{2,1,0:T(4,128)(2,1)} %select_select_fusion.1), calls=%async_computation | async-start | bytes 2097152 | tf_op jit(solution)/shard_map/all_to_all | solution.py:65
  1008.0 0.2 fusion.42
  1008.4 1.0 fusion.34
  1009.4 1.6 fusion.37
  1010.9 23.4 %all-to-all-done = bf16[32,4,4096]{2,1,0:T(4,128)(2,1)S(1)} async-done(((bf16[32,4,4096]{2,1,0:T(4,128)(2,1)}), bf16[32,4,4096]{2,1,0:T(4,128)(2,1)S(1)}, u32[]{:S(2)}, u32[]{:S(2)}) %all-to-all-start) | async-done | bytes 1048608 | tf_op jit(solution)/shard_map/all_to_all | solution.py:65
  1034.4 0.5 reshape.321
  1034.9 0.7 gather_fusion.2
  1035.7 1.3 collective-permute-start
  1037.0 1.5 dynamic-slice_bitcast_fusion
  1038.5 8.2 collective-permute-done
  1046.6 0.6 copy.72
  (101 shorter events, 4.0 us)
Async XLA Ops:
  7.2 14.2 %collective-permute-start.1 = (bf16[8,4096]{1,0:T(8,128)(2,1)}, bf16[8,4096]{1,0:T(8,128)(2,1)S(1)}, u32[]{:S(2)}, u32[]{:S(2)}) collective-permute-start(bf16[8,4096]{1,0:T(8,128)(2,1)} %bitcast.133), channel_id=1, source_target_pairs={{0,224},{32,0},{64,32},{96,64},{128,96},{160,128},{192,160},{224,1... | collective-permute-start | bytes 196616 | tf_op jit(solution)/shard_map/ppermute | solution.py:13
  24.0 9.9 copy-start.9
  24.1 9.9 copy-start.10
  24.1 9.9 copy-start.11
  26.3 34.4 %all-to-all-start.1 = ((bf16[32,4,4096]{2,1,0:T(4,128)(2,1)}), bf16[32,4,4096]{2,1,0:T(4,128)(2,1)S(1)}, u32[]{:S(2)}, u32[]{:S(2)}) async-start(bf16[32,4,4096]{2,1,0:T(4,128)(2,1)} %select_select_fusion), calls=%async_computation.1 | async-start | bytes 2097152 | tf_op jit(solution)/shard_map/all_to_all | solution.py:65
  33.9 61.1 %all-gather.7.cloned.1.call-start = ((), (), s32[]{:S(2)}) async-start(), calls=%async_computation.2 | async-start | bytes 1081344 | tf_op jit(solution)/shard_map/all_gather | solution.py:55
  34.7 119.7 %all-gather.9.cloned.1.call-start = ((), (), s32[]{:S(2)}) async-start(), calls=%async_computation.3 | async-start | bytes 1081344 | tf_op jit(solution)/shard_map/all_gather | solution.py:55
  62.6 622.6 %all-gather.11.cloned.1.call-start = ((), (), s32[]{:S(2)}) async-start(), calls=%async_computation.4 | async-start | bytes 1081344 | tf_op jit(solution)/shard_map/all_gather | solution.py:55
  96.3 3.3 copy-start.6
  155.7 3.3 copy-start.4
  159.1 2.0 copy-start.7
  160.2 2.0 copy-start.2
  162.2 4.1 copy-start
  166.4 531.5 %collective-permute-start.2 = (bf16[2,4096,448]{1,2,0:T(8,128)(2,1)}, bf16[2,4096,448]{1,2,0:T(8,128)(2,1)}, u32[]{:S(2)}, u32[]{:S(2)}) collective-permute-start(bf16[2,4096,448]{1,2,0:T(8,128)(2,1)} %pad_maximum_fusion), channel_id=1, source_target_pairs={{0,128},{32,160},{64,192},{96,224},{128,0},{160,32},{192,64},{224,... | collective-permute-start | bytes 22020104 | tf_op jit(solution)/shard_map/ppermute | solution.py:13
  170.0 804.8 %all-reduce.6.cloned.1.call-start = ((), (), s32[]{:S(2)}) async-start(), calls=%async_computation.5 | async-start | bytes 6291456
  175.0 526.7 %collective-permute-start.3 = (bf16[448,4096]{1,0:T(8,128)(2,1)}, bf16[448,4096]{1,0:T(8,128)(2,1)}, u32[]{:S(2)}, u32[]{:S(2)}) collective-permute-start(bf16[448,4096]{1,0:T(8,128)(2,1)} %subtract_convert_fusion), channel_id=1, source_target_pairs={{0,128},{32,160},{64,192},{96,224},{128,0},{160,32},{192,64},{224,... | collective-permute-start | bytes 11010056 | tf_op jit(solution)/shard_map/ppermute | solution.py:13
  686.6 4.2 copy-start.3
  689.6 2.5 copy-start.1
  692.0 2.0 copy-start.5
  694.1 2.0 copy-start.8
  711.4 1.5 copy-start.12
  980.6 53.8 %all-to-all-start = ((bf16[32,4,4096]{2,1,0:T(4,128)(2,1)}), bf16[32,4,4096]{2,1,0:T(4,128)(2,1)S(1)}, u32[]{:S(2)}, u32[]{:S(2)}) async-start(bf16[32,4,4096]{2,1,0:T(4,128)(2,1)} %select_select_fusion.1), calls=%async_computation | async-start | bytes 2097152 | tf_op jit(solution)/shard_map/all_to_all | solution.py:65
  1035.7 10.9 %collective-permute-start = (bf16[8,4096]{1,0:T(8,128)(2,1)S(1)}, bf16[8,4096]{1,0:T(8,128)(2,1)S(1)}, u32[]{:S(2)}, u32[]{:S(2)}) collective-permute-start(bf16[8,4096]{1,0:T(8,128)(2,1)S(1)} %select_select_fusion.2), channel_id=1, source_target_pairs={{0,32},{32,64},{64,96},{96,128},{128,160},{160,192},{192,224},{224... | collective-permute-start | bytes 196616 | tf_op jit(solution)/shard_map/ppermute | solution.py:13
Sparse Core Ops, SparseCore 0:
  37.2 57.7 all-gather.6
  97.4 56.9 all-gather.8
  170.2 515.0 all-gather.10
  709.9 264.9 all-reduce.5
where the time goes:
time: 1050 us
  waiting for transfers between devices  911 us (87%)
  starting transfers between devices  49.9 us (5%)
  matrix products  33.3 us (3%)
  local copies, waits for them, and re-layouts  26.3 us (3%)
  other arithmetic  18.6 us (2%)
  between operations  14.9 us (1%)
    all_gather x3, waiting for transfers between devices, gather_rows(): return lax.all_gather(local_rows, 'rep', axis=0, tiled=True)  594 us
    unnamed x5, waiting for transfers between devices  261 us
    all_to_all x2, waiting for transfers between devices, route_blocks(): lax.all_to_all(buffer_rows, 'rep', split_axis=0, concat_axis=0, tiled=True)  47.6 us
    all_to_all x2, starting transfers between devices, route_blocks(): lax.all_to_all(buffer_rows, 'rep', split_axis=0, concat_axis=0, tiled=True)  34.6 us
  transfers between devices with their start and end apart: 10, of which 7 were waited for; matrix products, arithmetic and copies ran while one was open for 4% of the time, Pallas kernels for 0%

commit v1 on v0

--- a/solution.py
+++ b/solution.py
@@ -6,6 +6,13 @@
 BLK = 2
 epsilon = 1e-05
 step_rate = 0.5
+
+
+def all_by_exchange(x, mesh_axis, dim):
+    devices = lax.axis_size(mesh_axis)
+    pieces = jnp.stack([x for _ in range(devices)])
+    pieces = lax.all_to_all(pieces, mesh_axis, split_axis=0, concat_axis=0)
+    return jnp.concatenate(pieces, axis=dim)
 
 
 def passed_along(value, axis, by):
@@ -52,7 +59,7 @@
 
 
 def gather_rows(local_rows):
-    return lax.all_gather(local_rows, "rep", axis=0, tiled=True)
+    return all_by_exchange(local_rows, "rep", 0)
 
 
 def reduce_rows(term_rows):

time: 1050 us -> 1000 us (0.952)
  waiting for transfers between devices: 911 us -> 844 us
  starting transfers between devices: 49.9 us -> 65 us
    all_gather x3 -> x0, waiting for transfers between devices: 594 us -> none  [gather_rows(): return lax.all_gather(local_rows, 'rep', axis=0, tiled=True)]
    all_to_all x0 -> x3, waiting for transfers between devices: none -> 526 us  [all_by_exchange(): pieces = lax.all_to_all(pieces, mesh_axis, split_axis=0, concat_axis=0)]
    all_to_all x0 -> x3, starting transfers between devices: none -> 15.4 us  [all_by_exchange(): pieces = lax.all_to_all(pieces, mesh_axis, split_axis=0, concat_axis=0)]
    unnamed x5 -> x2, waiting for transfers between devices: 261 us -> 260 us
where the time goes in v1:
time: 1000 us
  waiting for transfers between devices  844 us (84%)
  starting transfers between devices  65 us (6%)
  matrix products  35.1 us (4%)
  local copies, waits for them, and re-layouts  27.6 us (3%)
  other arithmetic  15.8 us (2%)
  between operations  15.2 us (2%)
    all_to_all x3, waiting for transfers between devices, all_by_exchange(): pieces = lax.all_to_all(pieces, mesh_axis, split_axis=0, concat_axis=0)  526 us
    unnamed x2, waiting for transfers between devices  260 us
    all_to_all x2, waiting for transfers between devices, route_blocks(): lax.all_to_all(buffer_rows, 'rep', split_axis=0, concat_axis=0, tiled=True)  49.8 us
    all_to_all x2, starting transfers between devices, route_blocks(): lax.all_to_all(buffer_rows, 'rep', split_axis=0, concat_axis=0, tiled=True)  34.6 us
  transfers between devices with their start and end apart: 10, of which 7 were waited for; matrix products, arithmetic and copies ran while one was open for 4% of the time, Pallas kernels for 0%

profile of v1, /device:TPU:33, one launch (start us, length us, event | category | flops | bytes accessed | tf_op | source)
XLA Modules:
  0.0 1002.9 jit_solution(122088677672634447)
XLA Ops:
  7.2 8.3 collective-permute-start.1
  15.4 0.8 reduce_window_sum.22
  16.2 0.9 reduce_window_sum.23
  17.1 0.9 dynamic-slice_reduce_fusion.1
  18.0 0.7 bitcast_subtract_fusion
  19.5 2.7 gather_fusion.4
  22.2 0.4 gather.37
  22.7 1.7 select_select_fusion
  24.4 7.6 all-to-all-start.2
  32.5 26.3 %all-to-all-done.2 = bf16[32,4,4096]{2,1,0:T(4,128)(2,1)S(1)} async-done(((bf16[32,4,4096]{2,1,0:T(4,128)(2,1)}), bf16[32,4,4096]{2,1,0:T(4,128)(2,1)S(1)}, u32[]{:S(2)}, u32[]{:S(2)}) %all-to-all-start.2) | async-done | bytes 1048608 | tf_op jit(solution)/shard_map/all_to_all | solution.py:72
  58.8 1.5 stack.17
  60.3 5.0 all-to-all-start
  65.6 0.8 gather_fusion.3
  67.0 0.6 reshape.365
  67.6 0.6 gather_fusion.5
  68.3 23.7 %all-to-all-done = bf16[32,4,4096]{2,1,0:T(4,128)(2,1)S(1)} async-done(((bf16[32,4,4096]{2,1,0:T(4,128)(2,1)}), bf16[32,4,4096]{2,1,0:T(4,128)(2,1)S(1)}, u32[]{:S(2)}, u32[]{:S(2)}) %all-to-all-start) | async-done | bytes 1048608 | tf_op jit(solution)/shard_map/all_to_all | solution.py:14
  92.1 1.5 stack.18
  93.5 5.1 all-to-all-start.3
  98.6 0.3 reshape.361
  98.9 4.0 fusion.13
  102.9 1.8 fusion.9
  104.7 20.6 %all-to-all-done.3 = bf16[32,4,4096]{2,1,0:T(4,128)(2,1)S(1)} async-done(((bf16[32,4,4096]{2,1,0:T(4,128)(2,1)}), bf16[32,4,4096]{2,1,0:T(4,128)(2,1)S(1)}, u32[]{:S(2)}, u32[]{:S(2)}) %all-to-all-start.3) | async-done | bytes 1048608 | tf_op jit(solution)/shard_map/all_to_all | solution.py:14
  125.3 0.3 reshape.366
  125.6 3.7 multiply_convert_fusion.3
  129.4 1.1 subtract_convert_fusion.2
  130.5 0.9 copy-done.7
  131.4 1.1 subtract_convert_fusion.1
  132.5 4.0 pad_maximum_fusion
  136.6 1.2 collective-permute-start.2
  137.8 1.5 stack.20
  139.3 5.3 all-to-all-start.4
  144.7 4.9 subtract_convert_fusion
  149.6 4.2 collective-permute-start.3
  153.8 481.6 %all-to-all-done.4 = bf16[32,4,4096]{2,1,0:T(4,128)(2,1)S(1)} async-done(((bf16[32,4,4096]{2,1,0:T(4,128)(2,1)}), bf16[32,4,4096]{2,1,0:T(4,128)(2,1)S(1)}, u32[]{:S(2)}, u32[]{:S(2)}) %all-to-all-start.4) | async-done | bytes 1048608 | tf_op jit(solution)/shard_map/all_to_all | solution.py:14
  635.4 0.3 reshape.367
  635.7 2.9 fusion.6
  638.7 1.2 convert_element_type.99
  639.9 1.1 fusion.61
  641.1 1.1 fusion.62
  642.3 0.9 copy-done.5
  643.2 0.8 fusion.11
  643.9 1.3 copy-done.8
  645.2 1.8 fusion
  647.0 3.9 fusion.17
  650.9 6.9 fusion.1
  657.8 1.1 convert_element_type.121
  659.3 0.7 fusion.53
  660.5 1.3 gather_fusion
  662.0 0.6 dynamic-slice.2
  663.3 260.3 %all-reduce.6.cloned.1.call-done = (bf16[128,4096]{1,0:T(8,128)(2,1)}, bf16[128,4096]{1,0:T(8,128)(2,1)}, bf16[128,4096]{1,0:T(8,128)(2,1)}) async-done(((bf16[128,4096]{1,0:T(8,128)(2,1)}, bf16[128,4096]{1,0:T(8,128)(2,1)}, bf16[128,4096]{1,0:T(8,128)(2,1)}), (bf16[128,4096]{1,0:T(8,128)(2,1)}, bf16[128,4096]{1,0:T(8,128)(2,1)}, bf16[128,4096]{1,0:T(8,128)(2,1)})) %all-reduce.6.cloned.1.call-update) | async-done | bytes 3145744
  923.6 0.9 constant_dynamic-slice_fusion.5
  924.5 2.7 gather_fusion.1
  927.2 0.4 gather.32
  927.6 1.7 select_select_fusion.1
  929.4 27.0 %all-to-all-start.1 = ((bf16[32,4,4096]{2,1,0:T(4,128)(2,1)}), bf16[32,4,4096]{2,1,0:T(4,128)(2,1)S(1)}, u32[]{:S(2)}, u32[]{:S(2)}) async-start(bf16[32,4,4096]{2,1,0:T(4,128)(2,1)} %select_select_fusion.1), calls=%async_computation.1 | async-start | bytes 2097152 | tf_op jit(solution)/shard_map/all_to_all | solution.py:72
  957.1 1.0 fusion.34
  958.1 1.6 fusion.43
  959.7 23.4 %all-to-all-done.1 = bf16[32,4,4096]{2,1,0:T(4,128)(2,1)S(1)} async-done(((bf16[32,4,4096]{2,1,0:T(4,128)(2,1)}), bf16[32,4,4096]{2,1,0:T(4,128)(2,1)S(1)}, u32[]{:S(2)}, u32[]{:S(2)}) %all-to-all-start.1) | async-done | bytes 1048608 | tf_op jit(solution)/shard_map/all_to_all | solution.py:72
  983.1 0.5 reshape.363
  983.7 0.7 gather_fusion.2
  984.5 1.3 collective-permute-start
  985.7 1.5 dynamic-slice_bitcast_fusion
  987.2 8.2 collective-permute-done
  995.4 0.6 copy.72
  (104 shorter events, 4.6 us)
Async XLA Ops:
  7.2 12.3 %collective-permute-start.1 = (bf16[8,4096]{1,0:T(8,128)(2,1)}, bf16[8,4096]{1,0:T(8,128)(2,1)S(1)}, u32[]{:S(2)}, u32[]{:S(2)}) collective-permute-start(bf16[8,4096]{1,0:T(8,128)(2,1)} %bitcast.151), channel_id=1, source_target_pairs={{0,224},{32,0},{64,32},{96,64},{128,96},{160,128},{192,160},{224,1... | collective-permute-start | bytes 196616 | tf_op jit(solution)/shard_map/ppermute | solution.py:20
  22.2 9.8 copy-start.11
  22.2 10.0 copy-start.12
  22.2 10.1 %copy-start.13 = (f32[1,4096]{1,0:T(1,128)S(1)}, f32[1,4096]{1,0:T(1,128)}, u32[]{:S(2)}) copy-start(f32[1,4096]{1,0:T(1,128)} %param.11) | copy-start | bytes 49156
  24.4 34.4 %all-to-all-start.2 = ((bf16[32,4,4096]{2,1,0:T(4,128)(2,1)}), bf16[32,4,4096]{2,1,0:T(4,128)(2,1)S(1)}, u32[]{:S(2)}, u32[]{:S(2)}) async-start(bf16[32,4,4096]{2,1,0:T(4,128)(2,1)} %select_select_fusion), calls=%async_computation.2 | async-start | bytes 2097152 | tf_op jit(solution)/shard_map/all_to_all | solution.py:72
  60.3 31.8 %all-to-all-start = ((bf16[32,4,4096]{2,1,0:T(4,128)(2,1)}), bf16[32,4,4096]{2,1,0:T(4,128)(2,1)S(1)}, u32[]{:S(2)}, u32[]{:S(2)}) async-start(bf16[32,4,4096]{2,1,0:T(4,128)(2,1)} %stack.17), calls=%async_computation | async-start | bytes 2097152 | tf_op jit(solution)/shard_map/all_to_all | solution.py:14
  93.5 31.8 %all-to-all-start.3 = ((bf16[32,4,4096]{2,1,0:T(4,128)(2,1)}), bf16[32,4,4096]{2,1,0:T(4,128)(2,1)S(1)}, u32[]{:S(2)}, u32[]{:S(2)}) async-start(bf16[32,4,4096]{2,1,0:T(4,128)(2,1)} %stack.18), calls=%async_computation.3 | async-start | bytes 2097152 | tf_op jit(solution)/shard_map/all_to_all | solution.py:14
  98.9 4.0 copy-start.6
  125.6 4.9 copy-start.9
  125.6 3.7 copy-start.4
  129.3 2.0 copy-start.7
  130.5 2.0 copy-start.2
  132.5 4.1 copy-start
  136.6 8.0 copy-start.10
  136.6 510.4 %collective-permute-start.2 = (bf16[2,4096,448]{1,2,0:T(8,128)(2,1)}, bf16[2,4096,448]{1,2,0:T(8,128)(2,1)}, u32[]{:S(2)}, u32[]{:S(2)}) collective-permute-start(bf16[2,4096,448]{1,2,0:T(8,128)(2,1)} %pad_maximum_fusion), channel_id=1, source_target_pairs={{0,128},{32,160},{64,192},{96,224},{128,0},{160,32},{192,64},{224,... | collective-permute-start | bytes 22020104 | tf_op jit(solution)/shard_map/ppermute | solution.py:20
  139.3 496.1 %all-to-all-start.4 = ((bf16[32,4,4096]{2,1,0:T(4,128)(2,1)}), bf16[32,4,4096]{2,1,0:T(4,128)(2,1)S(1)}, u32[]{:S(2)}, u32[]{:S(2)}) async-start(bf16[32,4,4096]{2,1,0:T(4,128)(2,1)} %stack.20), calls=%async_computation.4 | async-start | bytes 2097152 | tf_op jit(solution)/shard_map/all_to_all | solution.py:14
  144.6 779.0 %all-reduce.6.cloned.1.call-start = ((), (), s32[]{:S(2)}) async-start(), calls=%async_computation.5 | async-start | bytes 6291456
  149.6 501.2 %collective-permute-start.3 = (bf16[448,4096]{1,0:T(8,128)(2,1)}, bf16[448,4096]{1,0:T(8,128)(2,1)}, u32[]{:S(2)}, u32[]{:S(2)}) collective-permute-start(bf16[448,4096]{1,0:T(8,128)(2,1)} %subtract_convert_fusion), channel_id=1, source_target_pairs={{0,128},{32,160},{64,192},{96,224},{128,0},{160,32},{192,64},{224,... | collective-permute-start | bytes 11010056 | tf_op jit(solution)/shard_map/ppermute | solution.py:20
  635.7 4.2 copy-start.3
  638.7 2.5 copy-start.1
  641.1 2.0 copy-start.5
  643.2 2.0 copy-start.8
  660.5 1.5 copy-start.14
  929.4 53.8 %all-to-all-start.1 = ((bf16[32,4,4096]{2,1,0:T(4,128)(2,1)}), bf16[32,4,4096]{2,1,0:T(4,128)(2,1)S(1)}, u32[]{:S(2)}, u32[]{:S(2)}) async-start(bf16[32,4,4096]{2,1,0:T(4,128)(2,1)} %select_select_fusion.1), calls=%async_computation.1 | async-start | bytes 2097152 | tf_op jit(solution)/shard_map/all_to_all | solution.py:72
  984.5 10.9 %collective-permute-start = (bf16[8,4096]{1,0:T(8,128)(2,1)S(1)}, bf16[8,4096]{1,0:T(8,128)(2,1)S(1)}, u32[]{:S(2)}, u32[]{:S(2)}) collective-permute-start(bf16[8,4096]{1,0:T(8,128)(2,1)S(1)} %select_select_fusion.2), channel_id=1, source_target_pairs={{0,32},{32,64},{64,96},{96,128},{128,160},{160,192},{192,224},{224... | collective-permute-start | bytes 196616 | tf_op jit(solution)/shard_map/ppermute | solution.py:20
Sparse Core Ops, SparseCore 0:
  659.0 264.5 all-reduce.5
